TPU v7x, 32 devices: a whole 2x2x4 slice. The times are simulated.
32 devices in a mesh: gx: 4 (over y, x), gy: 2 (over core), gz: 4 (over z).
Axes of the slice: x: 2, y: 2, z: 4, core: 2. Of those that a mesh axis runs over, the one named last changes fastest.
Arguments:
- load_vector: float32 [32, 32, 2048], P(('gx', 'gy', 'gz')), may hold values from -24 to 24
- matrix_tiles: float32 [512, 7, 128, 128], P(('gx', 'gy', 'gz')), may hold values from -1 to 6, as said below
- tile_cols: int32 [512, 7], P(('gx', 'gy', 'gz')), may hold values from 0 to 15, as said below
- interior_inv: float32 [384, 128, 128], P(('gx', 'gy', 'gz')), may hold values from -0.1 to 0.3, as said below
- schur_inv: float32 [32, 512, 512], P(('gx', 'gy', 'gz')), may hold values from -0.1 to 0.3, as said below
- coarse_basis: float32 [32, 128, 2048], P(('gx', 'gy', 'gz')), may hold values from -0.125 to 0.125
- coarse_inv: float32 [32, 256, 256], P(('gx', 'gy', 'gz')), may hold values from -0.2 to 0.8, as said below
- row_map: int32 [32, 4, 128], P(('gx', 'gy', 'gz')), may hold values from 0 to 127, each once within a row
- face_link: int32 [32, 4], P(('gx', 'gy', 'gz')), may hold values from 0 to 1, as said below
- coarse_id: int32 [32, 4], P(('gx', 'gy', 'gz')), may hold values from 0 to 31, as said below
Outputs:
- solution: float32 [32, 32, 2048], P(('gx', 'gy', 'gz'))
- residual: float32 [32, 32, 2048], P(('gx', 'gy', 'gz'))
Inputs may be any that keep to these rules, and one draw needn't show every extreme that they name: `matrix_tiles`: tile 0 of each block row is its diagonal tile; each subdomain's matrix is symmetric positive definite: the tile of block row i in column block j is the transpose of the tile of block row j in column block i. `tile_cols`: tile 0 of block row i sits in column block i; tiles 1 to 6 sit in column blocks i + a, i - a, i + b, i - b, i + c, i - c modulo 16, for three distinct offsets a, b, c of that subdomain between 1 and (15) // 2; every column block holds exactly 7 tiles. `interior_inv`: each block is symmetric positive definite. `schur_inv`: symmetric positive definite. `coarse_inv`: symmetric positive definite. For partners d and e of round r, entry k of row_map[d, r] and of row_map[e, r] name the same shared unknown. `face_link`: equal for the two partners of a round. coarse_id = owner * 8 + slot, owner being a gz index within the subdomain's line of 4 devices; blocks with the same target are summed. Each subdomain sends at most 2 blocks to one owner and exactly 2 to some owner.
All inputs are finite; a program needn't handle non-finite values.
Results may differ from a plain program's by a relative error of at most 0.00018.
Values sent between devices are 32-bit elements; how exact they have to be, the bound alone decides.
No kernel may reach another device: no remote copies, remote signals or barrier semaphores. Data moves between devices by JAX's collectives and lax.ppermute only.
A program may use at most 64 MiB of HBM per device.

v0:
```python
import jax
import jax.numpy as jnp
from jax import lax
from jax.sharding import PartitionSpec as P

BS = 128
NIN = 12
NRHS = 32
CW = 32
CB = 4
OCAP = 8
ITERS = 2
NB = 16
NL = 2048
HIGH = lax.Precision.HIGHEST


def partner(value, axis, distance):
    return lax.ppermute(value, axis, [(i, i ^ 1 << distance) for i in range(lax.axis_size(axis))])


def on_device(
    load_vector,
    matrix_tiles,
    tile_cols,
    interior_inv,
    schur_inv,
    coarse_basis,
    coarse_inv,
    row_map,
    face_link,
    coarse_id,
):
    load_rows = load_vector[0]
    link_vals = face_link[0]
    face_maps = row_map[0]
    basis_rows = coarse_basis[0]
    schur_mat = schur_inv[0]
    coarse_mat = coarse_inv[0]
    block_ids = coarse_id[0]
    offset = NIN * BS
    line_size = lax.axis_size("gz")
    depth_z = line_size.bit_length() - 1
    depth_y = lax.axis_size("gy").bit_length() - 1
    swap_bits = [0, 1, depth_z, depth_z + depth_y]
    link_float = link_vals.astype(jnp.float32)
    weight = jnp.concatenate(
        [jnp.ones((offset,), jnp.float32)]
        + [jnp.broadcast_to(1.0 - 0.5 * link_float[round_no], (BS,)) for round_no in range(4)]
    )
    lane_ids = jnp.arange(BS, dtype=jnp.int32)
    onehots = [
        (face_maps[round_no][:, None] == lane_ids[None, :]).astype(jnp.float32)
        for round_no in range(4)
    ]

    def assemble(vector):
        outgoing = []
        for round_no in range(4):
            face_rows = vector[:, offset + round_no * BS : offset + (round_no + 1) * BS]
            outgoing.append(jnp.einsum("nj,kj->nk", face_rows, onehots[round_no], precision=HIGH))
        pieces = [vector[:, :offset]]
        for round_no in range(4):
            incoming = partner(outgoing[round_no], ("gx", "gy", "gz"), swap_bits[round_no])
            returned = jnp.dot(incoming, onehots[round_no], precision=HIGH)
            face_rows = vector[:, offset + round_no * BS : offset + (round_no + 1) * BS]
            pieces.append(face_rows + link_float[round_no] * returned)
        return jnp.concatenate(pieces, axis=1)

    group_rows = jnp.arange(line_size * OCAP, dtype=jnp.int32)
    dense_map = (group_rows[:, None] == block_ids[None, :]).astype(jnp.float32)

    def coarse_solve(summed):
        flat_rows = summed.reshape(OCAP * CW, NRHS)
        return jnp.dot(coarse_mat, flat_rows, precision=HIGH).reshape(OCAP, CW * NRHS)

    def coarse_part(contrib):
        summed = lax.psum_scatter(
            jnp.dot(dense_map, contrib, precision=HIGH), "gz", scatter_dimension=0, tiled=True
        )
        solved = coarse_solve(summed)
        all_solved = lax.all_gather(solved, "gz", axis=0, tiled=True)
        return jnp.einsum("ab,ac->bc", dense_map, all_solved, precision=HIGH)

    def precondition(resid):
        scaled = weight * resid
        inner_part = jnp.einsum(
            "bij,nbj->nbi", interior_inv, scaled[:, :offset].reshape(NRHS, NIN, BS), precision=HIGH
        ).reshape(NRHS, offset)
        outer_part = jnp.einsum("ij,nj->ni", schur_mat, scaled[:, offset:], precision=HIGH)
        contrib = jnp.einsum("cl,nl->cn", basis_rows, scaled, precision=HIGH).reshape(CB, CW * NRHS)
        coarse_back = coarse_part(contrib).reshape(CB * CW, NRHS)
        correction = jnp.einsum("cn,cl->nl", coarse_back, basis_rows, precision=HIGH)
        return assemble(weight * (jnp.concatenate([inner_part, outer_part], axis=1) + correction))

    def local_dot(left, right):
        return jnp.sum(weight * left * right, axis=1)

    resid = assemble(load_rows)
    solution = jnp.zeros_like(resid)
    precond_res = precondition(resid)

    def global_rz(left, right):
        return lax.psum(local_dot(left, right), ("gx", "gy", "gz"))

    direction = precond_res
    rho_now = global_rz(resid, precond_res)
    for turn_no in range(ITERS):
        picked = direction.reshape(NRHS, NB, BS)[:, tile_cols]
        product = jnp.einsum("rtij,nrtj->nri", matrix_tiles, picked, precision=HIGH).reshape(
            NRHS, NL
        )
        product_dir = assemble(product)
        curve_sum = lax.psum(local_dot(direction, product_dir), ("gx", "gy", "gz"))
        step_len = (rho_now / curve_sum)[:, None]
        solution = solution + step_len * direction
        resid = resid - step_len * product_dir
        if turn_no + 1 < ITERS:
            precond_res = precondition(resid)
            rho_next = global_rz(resid, precond_res)
            direction = precond_res + (rho_next / rho_now)[:, None] * direction
            rho_now = rho_next
    return (solution[None], resid[None])


def solution(mesh):
    in_specs = (
        P(("gx", "gy", "gz"), None, None),
        P(("gx", "gy", "gz"), None, None, None),
        P(("gx", "gy", "gz"), None),
        P(("gx", "gy", "gz"), None, None),
        P(("gx", "gy", "gz"), None, None),
        P(("gx", "gy", "gz"), None, None),
        P(("gx", "gy", "gz"), None, None),
        P(("gx", "gy", "gz"), None, None),
        P(("gx", "gy", "gz"), None),
        P(("gx", "gy", "gz"), None),
    )
    out_specs = (P(("gx", "gy", "gz"), None, None), P(("gx", "gy", "gz"), None, None))
    return jax.shard_map(
        on_device, mesh=mesh, in_specs=in_specs, out_specs=out_specs, check_vma=False
    )
```

profile of v0, /device:TPU:0, one launch (start us, length us, event | category | flops | bytes accessed | tf_op | source)
XLA Modules:
  0.0 299.2 jit_solution(18162430448153305590)
XLA Ops:
  9.0 3.1 %collective-permute-start = (f32[32,128]{0,1:T(8,128)S(1)}, f32[32,128]{0,1:T(8,128)S(1)}, u32[]{:S(2)}, u32[]{:S(2)}) collective-permute-start(f32[32,128]{0,1:T(8,128)S(1)} %convolution_bitcast_fusion.7), channel_id=1, source_target_pairs={{0,1},{1,0},{2,3},{3,2},{4,5},{5,4},{6,7},{7,6},{8,9},{9,8},{10,11... | collective-permute-start | bytes 49160 | tf_op jit(solution)/shard_map/ppermute | solution.py:19
  13.1 2.7 collective-permute-start.1
  17.7 1.6 collective-permute-start.3
  20.2 1.6 bitcast_dynamic-update-slice_fusion.2
  26.6 1.5 constant_dynamic-update-slice_fusion.4
  28.2 1.7 constant_dynamic-update-slice_fusion.3
  29.9 1.6 constant_dynamic-update-slice_fusion.2
  31.5 2.2 constant_dynamic-update-slice_fusion.1
  35.8 1.5 fusion.97
  41.6 12.3 %reduce-scatter.3.cloned.1.call-done = f32[8,1024]{1,0:T(8,128)} async-done(((f32[32,1024]{1,0:T(8,128)}), f32[8,1024]{1,0:T(8,128)}) %reduce-scatter.3.cloned.1.call-update) | async-done | bytes 32784 | tf_op jit(solution)/shard_map/reduce_scatter | solution.py:78
  55.3 13.4 %all_gather.6 = f32[32,1024]{1,0:T(8,128)S(1)} all-gather(f32[8,1024]{1,0:T(8,128)S(1)} %reshape.579), channel_id=1, replica_groups=mesh['gx'=4,'gy'=2,'gz'=4] {'gz'}, dimensions={0}, use_global_device_ids=true | all-gather | bytes 163840 | tf_op jit(solution)/shard_map/all_gather | solution.py:82
  79.5 9.9 %convolution_bitcast_fusion.1 = f32[16,4,8,128]{3,2,1,0:T(8,128)S(1)} fusion(f32[32,16,7,128]{3,0,2,1:T(8,128)S(1)} %bitcast.200, f32[16,7,128,128]{3,2,1,0:T(8,128)} %param.11), kind=kOutput, calls=%fused_computation.7 | convolution fusion | flops 704643072 | bytes 9437184 | tf_op jit(solution)/shard_map/rtij,nrtj->nri/dot_general | solution.py:110
  91.2 2.0 collective-permute-start.8
  94.0 1.6 collective-permute-start.11
  102.3 39.3 %all-reduce = (f32[32]{0:T(128)S(1)}, f32[32]{0:T(128)S(1)}) all-reduce(f32[32]{0:T(128)S(1)} %get-tuple-element.3, f32[32]{0:T(128)S(1)} %get-tuple-element.2), channel_id=1, replica_groups=mesh['gx'=4,'gy'=2,'gz'=4] {'gx','gy','gz'}, use_global_device_ids=true, to_apply=%region_2.0 | all-reduce | flops 64 | bytes 512 | tf_op jit(solution)/shard_map/psum | solution.py:104
  144.2 1.5 fusion.95
  151.3 14.2 %reduce-scatter.5.cloned.1.call-done = f32[8,1024]{1,0:T(8,128)} async-done(((f32[32,1024]{1,0:T(8,128)}), f32[8,1024]{1,0:T(8,128)}) %reduce-scatter.5.cloned.1.call-update) | async-done | bytes 32784 | tf_op jit(solution)/shard_map/reduce_scatter | solution.py:78
  167.0 13.3 %all_gather.7 = f32[32,1024]{1,0:T(8,128)S(1)} all-gather(f32[8,1024]{1,0:T(8,128)S(1)} %reshape.587), channel_id=1, replica_groups=mesh['gx'=4,'gy'=2,'gz'=4] {'gz'}, dimensions={0}, use_global_device_ids=true | all-gather | bytes 163840 | tf_op jit(solution)/shard_map/all_gather | solution.py:82
  183.6 1.5 collective-permute-start.15
  190.5 40.7 %psum.30 = f32[32]{0:T(128)S(1)} all-reduce(f32[32]{0:T(128)S(1)} %multiply_reduce_fusion.1), channel_id=1, replica_groups=mesh['gx'=4,'gy'=2,'gz'=4] {'gx','gy','gz'}, use_global_device_ids=true, to_apply=%region_7.0 | all-reduce | flops 32 | bytes 256 | tf_op jit(solution)/shard_map/psum | solution.py:104
  232.0 9.9 %convolution_bitcast_fusion = f32[16,4,8,128]{3,2,1,0:T(8,128)S(1)} fusion(f32[32,16,7,128]{3,0,2,1:T(8,128)S(1)} %bitcast.199, f32[16,7,128,128]{3,2,1,0:T(8,128)} %param.11), kind=kOutput, calls=%fused_computation.6 | convolution fusion | flops 704643072 | bytes 9437184 | tf_op jit(solution)/shard_map/rtij,nrtj->nri/dot_general | solution.py:110
  243.2 2.1 collective-permute-start.17
  245.3 2.3 collective-permute-start.19
  251.3 40.0 %psum.31 = f32[32]{0:T(128)S(1)} all-reduce(f32[32]{0:T(128)S(1)} %multiply_reduce_fusion), channel_id=1, replica_groups=mesh['gx'=4,'gy'=2,'gz'=4] {'gx','gy','gz'}, use_global_device_ids=true, to_apply=%region_9.0 | all-reduce | flops 32 | bytes 256 | tf_op jit(solution)/shard_map/psum | solution.py:114
  (222 shorter events, 60.1 us)
Async XLA Ops:
  7.2 46.7 %reduce-scatter.3.cloned.1.call-start = ((), (), s32[]{:S(2)}) async-start(), calls=%async_computation.2 | async-start | bytes 163840 | tf_op jit(solution)/shard_map/reduce_scatter | solution.py:78
  9.0 17.6 %collective-permute-start = (f32[32,128]{0,1:T(8,128)S(1)}, f32[32,128]{0,1:T(8,128)S(1)}, u32[]{:S(2)}, u32[]{:S(2)}) collective-permute-start(f32[32,128]{0,1:T(8,128)S(1)} %convolution_bitcast_fusion.7), channel_id=1, source_target_pairs={{0,1},{1,0},{2,3},{3,2},{4,5},{5,4},{6,7},{7,6},{8,9},{9,8},{10,11... | collective-permute-start | bytes 49160 | tf_op jit(solution)/shard_map/ppermute | solution.py:19
  13.1 15.1 %collective-permute-start.1 = (f32[32,128]{0,1:T(8,128)S(1)}, f32[32,128]{0,1:T(8,128)S(1)}, u32[]{:S(2)}, u32[]{:S(2)}) collective-permute-start(f32[32,128]{0,1:T(8,128)S(1)} %convolution_bitcast_fusion.6), channel_id=1, source_target_pairs={{0,2},{1,3},{2,0},{3,1},{4,6},{5,7},{6,4},{7,5},{8,10},{9,11},{10,... | collective-permute-start | bytes 49160 | tf_op jit(solution)/shard_map/ppermute | solution.py:19
  16.7 13.2 %collective-permute-start.2 = (f32[32,128]{0,1:T(8,128)S(1)}, f32[32,128]{0,1:T(8,128)S(1)}, u32[]{:S(2)}, u32[]{:S(2)}) collective-permute-start(f32[32,128]{0,1:T(8,128)S(1)} %convolution_bitcast_fusion.5), channel_id=1, source_target_pairs={{0,4},{1,5},{2,6},{3,7},{4,0},{5,1},{6,2},{7,3},{8,12},{9,13},{10,... | collective-permute-start | bytes 49160 | tf_op jit(solution)/shard_map/ppermute | solution.py:19
  17.7 13.7 %collective-permute-start.3 = (f32[32,128]{0,1:T(8,128)S(1)}, f32[32,128]{0,1:T(8,128)S(1)}, u32[]{:S(2)}, u32[]{:S(2)}) collective-permute-start(f32[32,128]{0,1:T(8,128)S(1)} %convolution_bitcast_fusion.4), channel_id=1, source_target_pairs={{0,8},{1,9},{2,10},{3,11},{4,12},{5,13},{6,14},{7,15},{8,0},{9,1},... | collective-permute-start | bytes 49160 | tf_op jit(solution)/shard_map/ppermute | solution.py:19
  37.3 128.2 %reduce-scatter.5.cloned.1.call-start = ((), (), s32[]{:S(2)}) async-start(), calls=%async_computation.3 | async-start | bytes 163840 | tf_op jit(solution)/shard_map/reduce_scatter | solution.py:78
  71.2 3.7 %collective-permute-start.4 = (f32[32,128]{1,0:T(8,128)S(1)}, f32[32,128]{1,0:T(8,128)S(1)}, u32[]{:S(2)}, u32[]{:S(2)}) collective-permute-start(f32[32,128]{1,0:T(8,128)S(1)} %fusion.53), channel_id=1, source_target_pairs={{0,1},{1,0},{2,3},{3,2},{4,5},{5,4},{6,7},{7,6},{8,9},{9,8},{10,11... | collective-permute-start | bytes 49160 | tf_op jit(solution)/shard_map/ppermute | solution.py:19
  71.4 4.7 %collective-permute-start.5 = (f32[32,128]{1,0:T(8,128)S(1)}, f32[32,128]{1,0:T(8,128)S(1)}, u32[]{:S(2)}, u32[]{:S(2)}) collective-permute-start(f32[32,128]{1,0:T(8,128)S(1)} %fusion.49), channel_id=1, source_target_pairs={{0,2},{1,3},{2,0},{3,1},{4,6},{5,7},{6,4},{7,5},{8,10},{9,11},{10,... | collective-permute-start | bytes 49160 | tf_op jit(solution)/shard_map/ppermute | solution.py:19
  72.7 4.3 %collective-permute-start.6 = (f32[32,128]{1,0:T(8,128)S(1)}, f32[32,128]{1,0:T(8,128)S(1)}, u32[]{:S(2)}, u32[]{:S(2)}) collective-permute-start(f32[32,128]{1,0:T(8,128)S(1)} %fusion.45), channel_id=1, source_target_pairs={{0,4},{1,5},{2,6},{3,7},{4,0},{5,1},{6,2},{7,3},{8,12},{9,13},{10,... | collective-permute-start | bytes 49160 | tf_op jit(solution)/shard_map/ppermute | solution.py:19
  72.7 5.2 %collective-permute-start.7 = (f32[32,128]{1,0:T(8,128)S(1)}, f32[32,128]{1,0:T(8,128)S(1)}, u32[]{:S(2)}, u32[]{:S(2)}) collective-permute-start(f32[32,128]{1,0:T(8,128)S(1)} %fusion.41), channel_id=1, source_target_pairs={{0,8},{1,9},{2,10},{3,11},{4,12},{5,13},{6,14},{7,15},{8,0},{9,1},... | collective-permute-start | bytes 49160 | tf_op jit(solution)/shard_map/ppermute | solution.py:19
  91.2 6.8 %collective-permute-start.8 = (f32[32,128]{1,0:T(8,128)S(1)}, f32[32,128]{1,0:T(8,128)S(1)}, u32[]{:S(2)}, u32[]{:S(2)}) collective-permute-start(f32[32,128]{1,0:T(8,128)S(1)} %fusion.52), channel_id=1, source_target_pairs={{0,1},{1,0},{2,3},{3,2},{4,5},{5,4},{6,7},{7,6},{8,9},{9,8},{10,11... | collective-permute-start | bytes 49160 | tf_op jit(solution)/shard_map/ppermute | solution.py:19
  93.2 5.6 %collective-permute-start.9 = (f32[32,128]{1,0:T(8,128)S(1)}, f32[32,128]{1,0:T(8,128)S(1)}, u32[]{:S(2)}, u32[]{:S(2)}) collective-permute-start(f32[32,128]{1,0:T(8,128)S(1)} %fusion.48), channel_id=1, source_target_pairs={{0,2},{1,3},{2,0},{3,1},{4,6},{5,7},{6,4},{7,5},{8,10},{9,11},{10,... | collective-permute-start | bytes 49160 | tf_op jit(solution)/shard_map/ppermute | solution.py:19
  94.0 5.7 %collective-permute-start.10 = (f32[32,128]{1,0:T(8,128)S(1)}, f32[32,128]{1,0:T(8,128)S(1)}, u32[]{:S(2)}, u32[]{:S(2)}) collective-permute-start(f32[32,128]{1,0:T(8,128)S(1)} %fusion.44), channel_id=1, source_target_pairs={{0,4},{1,5},{2,6},{3,7},{4,0},{5,1},{6,2},{7,3},{8,12},{9,13},{10,... | collective-permute-start | bytes 49160 | tf_op jit(solution)/shard_map/ppermute | solution.py:19
  94.0 6.7 %collective-permute-start.11 = (f32[32,128]{1,0:T(8,128)S(1)}, f32[32,128]{1,0:T(8,128)S(1)}, u32[]{:S(2)}, u32[]{:S(2)}) collective-permute-start(f32[32,128]{1,0:T(8,128)S(1)} %fusion.40), channel_id=1, source_target_pairs={{0,8},{1,9},{2,10},{3,11},{4,12},{5,13},{6,14},{7,15},{8,0},{9,1},... | collective-permute-start | bytes 49160 | tf_op jit(solution)/shard_map/ppermute | solution.py:19
  180.3 50.8 %copy-start.31 = (f32[32]{0:T(128)S(1)}, f32[32]{0:T(128)}, u32[]{:S(2)}) copy-start(f32[32]{0:T(128)} %copy-done.30) | copy-start | bytes 388
  182.0 3.8 %collective-permute-start.12 = (f32[32,128]{1,0:T(8,128)S(1)}, f32[32,128]{1,0:T(8,128)S(1)}, u32[]{:S(2)}, u32[]{:S(2)}) collective-permute-start(f32[32,128]{1,0:T(8,128)S(1)} %fusion.51), channel_id=1, source_target_pairs={{0,1},{1,0},{2,3},{3,2},{4,5},{5,4},{6,7},{7,6},{8,9},{9,8},{10,11... | collective-permute-start | bytes 49160 | tf_op jit(solution)/shard_map/ppermute | solution.py:19
  182.3 4.7 %collective-permute-start.13 = (f32[32,128]{1,0:T(8,128)S(1)}, f32[32,128]{1,0:T(8,128)S(1)}, u32[]{:S(2)}, u32[]{:S(2)}) collective-permute-start(f32[32,128]{1,0:T(8,128)S(1)} %fusion.47), channel_id=1, source_target_pairs={{0,2},{1,3},{2,0},{3,1},{4,6},{5,7},{6,4},{7,5},{8,10},{9,11},{10,... | collective-permute-start | bytes 49160 | tf_op jit(solution)/shard_map/ppermute | solution.py:19
  183.6 4.3 %collective-permute-start.14 = (f32[32,128]{1,0:T(8,128)S(1)}, f32[32,128]{1,0:T(8,128)S(1)}, u32[]{:S(2)}, u32[]{:S(2)}) collective-permute-start(f32[32,128]{1,0:T(8,128)S(1)} %fusion.43), channel_id=1, source_target_pairs={{0,4},{1,5},{2,6},{3,7},{4,0},{5,1},{6,2},{7,3},{8,12},{9,13},{10,... | collective-permute-start | bytes 49160 | tf_op jit(solution)/shard_map/ppermute | solution.py:19
  183.6 5.2 %collective-permute-start.15 = (f32[32,128]{1,0:T(8,128)S(1)}, f32[32,128]{1,0:T(8,128)S(1)}, u32[]{:S(2)}, u32[]{:S(2)}) collective-permute-start(f32[32,128]{1,0:T(8,128)S(1)} %fusion.39), channel_id=1, source_target_pairs={{0,8},{1,9},{2,10},{3,11},{4,12},{5,13},{6,14},{7,15},{8,0},{9,1},... | collective-permute-start | bytes 49160 | tf_op jit(solution)/shard_map/ppermute | solution.py:19
  242.0 49.3 %copy-start.33 = (f32[32]{0:T(128)S(1)}, f32[32]{0:T(128)}, u32[]{:S(2)}) copy-start(f32[32]{0:T(128)} %copy-done.32) | copy-start | bytes 388
  243.1 4.5 %collective-permute-start.16 = (f32[32,128]{1,0:T(8,128)S(1)}, f32[32,128]{1,0:T(8,128)S(1)}, u32[]{:S(2)}, u32[]{:S(2)}) collective-permute-start(f32[32,128]{1,0:T(8,128)S(1)} %fusion.50), channel_id=1, source_target_pairs={{0,1},{1,0},{2,3},{3,2},{4,5},{5,4},{6,7},{7,6},{8,9},{9,8},{10,11... | collective-permute-start | bytes 49160 | tf_op jit(solution)/shard_map/ppermute | solution.py:19
  243.2 5.2 %collective-permute-start.17 = (f32[32,128]{1,0:T(8,128)S(1)}, f32[32,128]{1,0:T(8,128)S(1)}, u32[]{:S(2)}, u32[]{:S(2)}) collective-permute-start(f32[32,128]{1,0:T(8,128)S(1)} %fusion.46), channel_id=1, source_target_pairs={{0,2},{1,3},{2,0},{3,1},{4,6},{5,7},{6,4},{7,5},{8,10},{9,11},{10,... | collective-permute-start | bytes 49160 | tf_op jit(solution)/shard_map/ppermute | solution.py:19
  245.3 4.0 %collective-permute-start.18 = (f32[32,128]{1,0:T(8,128)S(1)}, f32[32,128]{1,0:T(8,128)S(1)}, u32[]{:S(2)}, u32[]{:S(2)}) collective-permute-start(f32[32,128]{1,0:T(8,128)S(1)} %fusion.42), channel_id=1, source_target_pairs={{0,4},{1,5},{2,6},{3,7},{4,0},{5,1},{6,2},{7,3},{8,12},{9,13},{10,... | collective-permute-start | bytes 49160 | tf_op jit(solution)/shard_map/ppermute | solution.py:19
  245.3 4.9 %collective-permute-start.19 = (f32[32,128]{1,0:T(8,128)S(1)}, f32[32,128]{1,0:T(8,128)S(1)}, u32[]{:S(2)}, u32[]{:S(2)}) collective-permute-start(f32[32,128]{1,0:T(8,128)S(1)} %fusion.38), channel_id=1, source_target_pairs={{0,8},{1,9},{2,10},{3,11},{4,12},{5,13},{6,14},{7,15},{8,0},{9,1},... | collective-permute-start | bytes 49160 | tf_op jit(solution)/shard_map/ppermute | solution.py:19
  (32 other events, 767.2 us)
Sparse Core Ops, SparseCore 0:
  37.4 16.4 reduce-scatter.2
  145.9 19.6 reduce-scatter.4
where the time goes:
time: 300 us; the launch traced here: 299 us
  blocking collectives  147 us (49%)
  matrix products  60.6 us (20%)
  waiting for transfers between devices  28.8 us (10%)
  starting transfers between devices  22 us (7%)
  local copies, waits for them, and re-layouts  20.4 us (7%)
  between operations  17.6 us (6%)
  other arithmetic  3.1 us (1%)
    psum x2, blocking collectives, global_rz(): return lax.psum(local_dot(left, right), ('gx', 'gy', 'gz'))  80 us
    psum x1, blocking collectives, on_device(): curve_sum = lax.psum(local_dot(direction, product_dir), ('gx', 'gy', 'gz'))  40 us
    all_gather x2, blocking collectives, coarse_part(): all_solved = lax.all_gather(solved, 'gz', axis=0, tiled=True)  26.7 us
    reduce_scatter x2, waiting for transfers between devices, coarse_part(): lax.psum_scatter(jnp.dot(dense_map, contrib, precision=HIGH), 'gz', scatt...  26.5 us
    ppermute x20, starting transfers between devices, partner(): lax.ppermute(value, axis, [(i, i ^ 1 << distance) for i in range(lax.axis...  21.9 us
    dot_general x20, matrix products, assemble(): returned = jnp.dot(incoming, onehots[round_no], precision=HIGH)  21 us
    dot_general x2, matrix products, on_device(): jnp.einsum('rtij,nrtj->nri', matrix_tiles, picked, precision=HIGH)  19.8 us
    unnamed x97, local copies, waits for them, and re-layouts  12.5 us
  transfers between devices with their start and end apart: 22, of which 6 were waited for; matrix products, arithmetic and copies ran while one was open for 12% of the time, Pallas kernels for 0%

commit v1 on v0

--- a/solution.py
+++ b/solution.py
@@ -13,6 +13,27 @@
 NB = 16
 NL = 2048
 HIGH = lax.Precision.HIGHEST
+
+
+def points_plan(xs, in_dim):
+    axis_tag = "gz"
+    parts_n = jax.lax.psum(1, axis_name=axis_tag)
+    gallery = []
+    for j in range(parts_n):
+        gallery.append((j, (j + 1) % parts_n))
+
+    def do_the_shifts_all(x_next):
+        if len(x_next) == parts_n:
+            return x_next
+        item_now = jax.lax.ppermute(x_next[0], axis_tag, perm=gallery)
+        tile_out = do_the_shifts_all([item_now, *x_next])
+        return tile_out
+
+    high = do_the_shifts_all([xs])
+    u_next = jnp.concatenate(high, in_dim)
+    view_out = jax.lax.axis_index(axis_tag)
+    aux = jnp.roll(u_next, (view_out + 1) * xs.shape[in_dim], in_dim)
+    return aux
 
 
 def partner(value, axis, distance):
@@ -79,7 +100,7 @@
             jnp.dot(dense_map, contrib, precision=HIGH), "gz", scatter_dimension=0, tiled=True
         )
         solved = coarse_solve(summed)
-        all_solved = lax.all_gather(solved, "gz", axis=0, tiled=True)
+        all_solved = points_plan(solved, 0)
         return jnp.einsum("ab,ac->bc", dense_map, all_solved, precision=HIGH)
 
     def precondition(resid):

time: 300 us -> 311 us (1.037)
  waiting for transfers between devices: 28.8 us -> 65.8 us
  blocking collectives: 147 us -> 118 us
    ppermute x0 -> x6, waiting for transfers between devices: none -> 29.7 us  [do_the_shifts_all(): item_now = jax.lax.ppermute(x_next[0], axis_tag, perm=gallery)]
    all_gather x2 -> x0, blocking collectives: 26.7 us -> none  [coarse_part(): all_solved = lax.all_gather(solved, 'gz', axis=0, tiled=True)]
    reduce_scatter x2, waiting for transfers between devices: 26.5 us -> 31.9 us  [coarse_part(): lax.psum_scatter(jnp.dot(dense_map, contrib, precision=HIGH), 'gz', scatt...]
    unnamed x97 -> x89, local copies, waits for them, and re-layouts: 12.5 us -> 14.5 us
  transfers between devices with their start and end apart: 22 -> 28, of which waited for: 6 -> 12; matrix products, arithmetic and copies ran while one was open for 12% -> 12% of each run, Pallas kernels for 0% -> 0%
where the time goes in v1:
time: 311 us; the launch traced here: 310 us
  blocking collectives  118 us (38%)
  waiting for transfers between devices  65.8 us (21%)
  matrix products  62.6 us (20%)
  local copies, waits for them, and re-layouts  22.3 us (7%)
  starting transfers between devices  19.7 us (6%)
  between operations  17.6 us (6%)
  other arithmetic  4.06 us (1%)
    psum x2, blocking collectives, global_rz(): return lax.psum(local_dot(left, right), ('gx', 'gy', 'gz'))  80.1 us
    psum x1, blocking collectives, on_device(): curve_sum = lax.psum(local_dot(direction, product_dir), ('gx', 'gy', 'gz'))  38 us
    reduce_scatter x2, waiting for transfers between devices, coarse_part(): lax.psum_scatter(jnp.dot(dense_map, contrib, precision=HIGH), 'gz', scatt...  31.9 us
    ppermute x6, waiting for transfers between devices, do_the_shifts_all(): item_now = jax.lax.ppermute(x_next[0], axis_tag, perm=gallery)  29.7 us
    dot_general x20, matrix products, assemble(): returned = jnp.dot(incoming, onehots[round_no], precision=HIGH)  21.1 us
    dot_general x2, matrix products, on_device(): jnp.einsum('rtij,nrtj->nri', matrix_tiles, picked, precision=HIGH)  19.8 us
    ppermute x20, starting transfers between devices, partner(): lax.ppermute(value, axis, [(i, i ^ 1 << distance) for i in range(lax.axis...  19.5 us
    unnamed x89, local copies, waits for them, and re-layouts  14.5 us
  transfers between devices with their start and end apart: 28, of which 12 were waited for; matrix products, arithmetic and copies ran while one was open for 12% of the time, Pallas kernels for 0%

profile of v1, /device:TPU:0, one launch (start us, length us, event | category | flops | bytes accessed | tf_op | source)
XLA Modules:
  0.0 310.1 jit_solution(13912677524515277889)
XLA Ops:
  9.0 3.1 collective-permute-start
  13.1 2.7 collective-permute-start.1
  20.2 1.7 bitcast_dynamic-update-slice_fusion.2
  26.7 1.7 constant_dynamic-update-slice_fusion.4
  31.5 2.3 constant_dynamic-update-slice_fusion.1
  38.4 14.9 %reduce-scatter.3.cloned.1.call-done = f32[8,1024]{1,0:T(8,128)} async-done(((f32[32,1024]{1,0:T(8,128)}), f32[8,1024]{1,0:T(8,128)}) %reduce-scatter.3.cloned.1.call-update) | async-done | bytes 32784 | tf_op jit(solution)/shard_map/reduce_scatter | solution.py:99
  56.4 5.1 %collective-permute-done.4 = f32[8,1024]{1,0:T(8,128)S(1)} collective-permute-done((f32[8,1024]{1,0:T(8,128)S(1)}, f32[8,1024]{1,0:T(8,128)S(1)}, u32[]{:S(2)}, u32[]{:S(2)}) %collective-permute-start.4) | collective-permute-done | bytes 32800 | tf_op jit(solution)/shard_map/ppermute | solution.py:28
  62.1 5.4 %collective-permute-done.5 = f32[8,1024]{1,0:T(8,128)S(1)} collective-permute-done((f32[8,1024]{1,0:T(8,128)S(1)}, f32[8,1024]{1,0:T(8,128)S(1)}, u32[]{:S(2)}, u32[]{:S(2)}) %collective-permute-start.5) | collective-permute-done | bytes 32800 | tf_op jit(solution)/shard_map/ppermute | solution.py:28
  68.9 4.3 %collective-permute-done.6 = f32[8,1024]{1,0:T(8,128)S(1)} collective-permute-done((f32[8,1024]{1,0:T(8,128)S(1)}, f32[8,1024]{1,0:T(8,128)S(1)}, u32[]{:S(2)}, u32[]{:S(2)}) %collective-permute-start.6) | collective-permute-done | bytes 32800 | tf_op jit(solution)/shard_map/ppermute | solution.py:28
  77.8 1.7 collective-permute-done.7
  84.0 9.9 %convolution_bitcast_fusion.1 = f32[16,4,8,128]{3,2,1,0:T(8,128)S(1)} fusion(f32[32,16,7,128]{3,0,2,1:T(8,128)S(1)} %bitcast.198, f32[16,7,128,128]{3,2,1,0:T(8,128)} %param.13), kind=kOutput, calls=%fused_computation.7 | convolution fusion | flops 704643072 | bytes 9437184 | tf_op jit(solution)/shard_map/rtij,nrtj->nri/dot_general | solution.py:131
  95.7 2.0 collective-permute-start.11
  106.4 39.6 %all-reduce = (f32[32]{0:T(128)S(1)}, f32[32]{0:T(128)S(1)}) all-reduce(f32[32]{0:T(128)S(1)} %get-tuple-element.4, f32[32]{0:T(128)S(1)} %get-tuple-element.3), channel_id=1, replica_groups=mesh['gx'=4,'gy'=2,'gz'=4] {'gx','gy','gz'}, use_global_device_ids=true, to_apply=%region_2.4 | all-reduce | flops 64 | bytes 512 | tf_op jit(solution)/shard_map/psum | solution.py:125
  153.1 17.0 %reduce-scatter.5.cloned.1.call-done = f32[8,1024]{1,0:T(8,128)} async-done(((f32[32,1024]{1,0:T(8,128)}), f32[8,1024]{1,0:T(8,128)}) %reduce-scatter.5.cloned.1.call-update) | async-done | bytes 32784 | tf_op jit(solution)/shard_map/reduce_scatter | solution.py:99
  173.2 5.1 %collective-permute-done.15 = f32[8,1024]{1,0:T(8,128)S(1)} collective-permute-done((f32[8,1024]{1,0:T(8,128)S(1)}, f32[8,1024]{1,0:T(8,128)S(1)}, u32[]{:S(2)}, u32[]{:S(2)}) %collective-permute-start.15) | collective-permute-done | bytes 32800 | tf_op jit(solution)/shard_map/ppermute | solution.py:28
  178.9 5.4 %collective-permute-done.16 = f32[8,1024]{1,0:T(8,128)S(1)} collective-permute-done((f32[8,1024]{1,0:T(8,128)S(1)}, f32[8,1024]{1,0:T(8,128)S(1)}, u32[]{:S(2)}, u32[]{:S(2)}) %collective-permute-start.16) | collective-permute-done | bytes 32800 | tf_op jit(solution)/shard_map/ppermute | solution.py:28
  185.7 4.3 %collective-permute-done.17 = f32[8,1024]{1,0:T(8,128)S(1)} collective-permute-done((f32[8,1024]{1,0:T(8,128)S(1)}, f32[8,1024]{1,0:T(8,128)S(1)}, u32[]{:S(2)}, u32[]{:S(2)}) %collective-permute-start.17) | collective-permute-done | bytes 32800 | tf_op jit(solution)/shard_map/ppermute | solution.py:28
  193.9 1.7 collective-permute-done.18
  200.2 40.5 %psum.30 = f32[32]{0:T(128)S(1)} all-reduce(f32[32]{0:T(128)S(1)} %multiply_reduce_fusion.1), channel_id=1, replica_groups=mesh['gx'=4,'gy'=2,'gz'=4] {'gx','gy','gz'}, use_global_device_ids=true, to_apply=%region_7.9 | all-reduce | flops 32 | bytes 256 | tf_op jit(solution)/shard_map/psum | solution.py:125
  241.6 9.9 %convolution_bitcast_fusion = f32[16,4,8,128]{3,2,1,0:T(8,128)S(1)} fusion(f32[32,16,7,128]{3,0,2,1:T(8,128)S(1)} %bitcast.197, f32[16,7,128,128]{3,2,1,0:T(8,128)} %param.13), kind=kOutput, calls=%fused_computation.6 | convolution fusion | flops 704643072 | bytes 9437184 | tf_op jit(solution)/shard_map/rtij,nrtj->nri/dot_general | solution.py:131
  252.7 2.2 collective-permute-start.23
  254.8 2.3 collective-permute-start.25
  263.3 38.0 %psum.31 = f32[32]{0:T(128)S(1)} all-reduce(f32[32]{0:T(128)S(1)} %multiply_reduce_fusion), channel_id=1, replica_groups=mesh['gx'=4,'gy'=2,'gz'=4] {'gx','gy','gz'}, use_global_device_ids=true, to_apply=%region_9.11 | all-reduce | flops 32 | bytes 256 | tf_op jit(solution)/shard_map/psum | solution.py:135
  301.4 1.9 multiply_subtract_fusion
  (224 shorter events, 69.8 us)
Async XLA Ops:
  7.2 46.1 %reduce-scatter.3.cloned.1.call-start = ((), (), s32[]{:S(2)}) async-start(), calls=%async_computation.2 | async-start | bytes 163840 | tf_op jit(solution)/shard_map/reduce_scatter | solution.py:99
  9.0 17.7 %collective-permute-start = (f32[32,128]{0,1:T(8,128)S(1)}, f32[32,128]{0,1:T(8,128)S(1)}, u32[]{:S(2)}, u32[]{:S(2)}) collective-permute-start(f32[32,128]{0,1:T(8,128)S(1)} %convolution_bitcast_fusion.7), channel_id=1, source_target_pairs={{0,1},{1,0},{2,3},{3,2},{4,5},{5,4},{6,7},{7,6},{8,9},{9,8},{10,11... | collective-permute-start | bytes 49160 | tf_op jit(solution)/shard_map/ppermute | solution.py:40
  13.1 15.3 %collective-permute-start.1 = (f32[32,128]{0,1:T(8,128)S(1)}, f32[32,128]{0,1:T(8,128)S(1)}, u32[]{:S(2)}, u32[]{:S(2)}) collective-permute-start(f32[32,128]{0,1:T(8,128)S(1)} %convolution_bitcast_fusion.6), channel_id=1, source_target_pairs={{0,2},{1,3},{2,0},{3,1},{4,6},{5,7},{6,4},{7,5},{8,10},{9,11},{10,... | collective-permute-start | bytes 49160 | tf_op jit(solution)/shard_map/ppermute | solution.py:40
  16.7 13.3 %collective-permute-start.2 = (f32[32,128]{0,1:T(8,128)S(1)}, f32[32,128]{0,1:T(8,128)S(1)}, u32[]{:S(2)}, u32[]{:S(2)}) collective-permute-start(f32[32,128]{0,1:T(8,128)S(1)} %convolution_bitcast_fusion.5), channel_id=1, source_target_pairs={{0,4},{1,5},{2,6},{3,7},{4,0},{5,1},{6,2},{7,3},{8,12},{9,13},{10,... | collective-permute-start | bytes 49160 | tf_op jit(solution)/shard_map/ppermute | solution.py:40
  17.7 13.8 %collective-permute-start.3 = (f32[32,128]{0,1:T(8,128)S(1)}, f32[32,128]{0,1:T(8,128)S(1)}, u32[]{:S(2)}, u32[]{:S(2)}) collective-permute-start(f32[32,128]{0,1:T(8,128)S(1)} %convolution_bitcast_fusion.4), channel_id=1, source_target_pairs={{0,8},{1,9},{2,10},{3,11},{4,12},{5,13},{6,14},{7,15},{8,0},{9,1},... | collective-permute-start | bytes 49160 | tf_op jit(solution)/shard_map/ppermute | solution.py:40
  36.7 133.4 %reduce-scatter.5.cloned.1.call-start = ((), (), s32[]{:S(2)}) async-start(), calls=%async_computation.3 | async-start | bytes 163840 | tf_op jit(solution)/shard_map/reduce_scatter | solution.py:99
  55.7 5.8 %collective-permute-start.4 = (f32[8,1024]{1,0:T(8,128)S(1)}, f32[8,1024]{1,0:T(8,128)S(1)}, u32[]{:S(2)}, u32[]{:S(2)}) collective-permute-start(f32[8,1024]{1,0:T(8,128)S(1)} %reshape.579), channel_id=1, source_target_pairs={{0,1},{1,2},{2,3},{3,0},{4,5},{5,6},{6,7},{7,4},{8,9},{9,10},{10,1... | collective-permute-start | bytes 98312 | tf_op jit(solution)/shard_map/ppermute | solution.py:28
  61.5 6.0 %collective-permute-start.5 = (f32[8,1024]{1,0:T(8,128)S(1)}, f32[8,1024]{1,0:T(8,128)S(1)}, u32[]{:S(2)}, u32[]{:S(2)}) collective-permute-start(f32[8,1024]{1,0:T(8,128)S(1)} %collective-permute-done.4), channel_id=1, source_target_pairs={{0,1},{1,2},{2,3},{3,0},{4,5},{5,6},{6,7},{7,4},{8,9},{9,10},{10,1... | collective-permute-start | bytes 98312 | tf_op jit(solution)/shard_map/ppermute | solution.py:28
  67.5 5.7 %collective-permute-start.6 = (f32[8,1024]{1,0:T(8,128)S(1)}, f32[8,1024]{1,0:T(8,128)S(1)}, u32[]{:S(2)}, u32[]{:S(2)}) collective-permute-start(f32[8,1024]{1,0:T(8,128)S(1)} %collective-permute-done.5), channel_id=1, source_target_pairs={{0,1},{1,2},{2,3},{3,0},{4,5},{5,6},{6,7},{7,4},{8,9},{9,10},{10,1... | collective-permute-start | bytes 98312 | tf_op jit(solution)/shard_map/ppermute | solution.py:28
  76.3 5.2 %collective-permute-start.9 = (f32[32,128]{1,0:T(8,128)S(1)}, f32[32,128]{1,0:T(8,128)S(1)}, u32[]{:S(2)}, u32[]{:S(2)}) collective-permute-start(f32[32,128]{1,0:T(8,128)S(1)} %fusion.65), channel_id=1, source_target_pairs={{0,4},{1,5},{2,6},{3,7},{4,0},{5,1},{6,2},{7,3},{8,12},{9,13},{10,... | collective-permute-start | bytes 49160 | tf_op jit(solution)/shard_map/ppermute | solution.py:40
  76.3 6.0 %collective-permute-start.10 = (f32[32,128]{1,0:T(8,128)S(1)}, f32[32,128]{1,0:T(8,128)S(1)}, u32[]{:S(2)}, u32[]{:S(2)}) collective-permute-start(f32[32,128]{1,0:T(8,128)S(1)} %fusion.61), channel_id=1, source_target_pairs={{0,8},{1,9},{2,10},{3,11},{4,12},{5,13},{6,14},{7,15},{8,0},{9,1},... | collective-permute-start | bytes 49160 | tf_op jit(solution)/shard_map/ppermute | solution.py:40
  95.7 6.4 %collective-permute-start.11 = (f32[32,128]{1,0:T(8,128)S(1)}, f32[32,128]{1,0:T(8,128)S(1)}, u32[]{:S(2)}, u32[]{:S(2)}) collective-permute-start(f32[32,128]{1,0:T(8,128)S(1)} %fusion.72), channel_id=1, source_target_pairs={{0,1},{1,0},{2,3},{3,2},{4,5},{5,4},{6,7},{7,6},{8,9},{9,8},{10,11... | collective-permute-start | bytes 49160 | tf_op jit(solution)/shard_map/ppermute | solution.py:40
  97.7 5.3 %collective-permute-start.12 = (f32[32,128]{1,0:T(8,128)S(1)}, f32[32,128]{1,0:T(8,128)S(1)}, u32[]{:S(2)}, u32[]{:S(2)}) collective-permute-start(f32[32,128]{1,0:T(8,128)S(1)} %fusion.68), channel_id=1, source_target_pairs={{0,2},{1,3},{2,0},{3,1},{4,6},{5,7},{6,4},{7,5},{8,10},{9,11},{10,... | collective-permute-start | bytes 49160 | tf_op jit(solution)/shard_map/ppermute | solution.py:40
  98.5 6.1 %collective-permute-start.13 = (f32[32,128]{1,0:T(8,128)S(1)}, f32[32,128]{1,0:T(8,128)S(1)}, u32[]{:S(2)}, u32[]{:S(2)}) collective-permute-start(f32[32,128]{1,0:T(8,128)S(1)} %fusion.64), channel_id=1, source_target_pairs={{0,4},{1,5},{2,6},{3,7},{4,0},{5,1},{6,2},{7,3},{8,12},{9,13},{10,... | collective-permute-start | bytes 49160 | tf_op jit(solution)/shard_map/ppermute | solution.py:40
  98.5 6.9 %collective-permute-start.14 = (f32[32,128]{1,0:T(8,128)S(1)}, f32[32,128]{1,0:T(8,128)S(1)}, u32[]{:S(2)}, u32[]{:S(2)}) collective-permute-start(f32[32,128]{1,0:T(8,128)S(1)} %fusion.60), channel_id=1, source_target_pairs={{0,8},{1,9},{2,10},{3,11},{4,12},{5,13},{6,14},{7,15},{8,0},{9,1},... | collective-permute-start | bytes 49160 | tf_op jit(solution)/shard_map/ppermute | solution.py:40
  172.5 5.8 %collective-permute-start.15 = (f32[8,1024]{1,0:T(8,128)S(1)}, f32[8,1024]{1,0:T(8,128)S(1)}, u32[]{:S(2)}, u32[]{:S(2)}) collective-permute-start(f32[8,1024]{1,0:T(8,128)S(1)} %reshape.587), channel_id=1, source_target_pairs={{0,1},{1,2},{2,3},{3,0},{4,5},{5,6},{6,7},{7,4},{8,9},{9,10},{10,1... | collective-permute-start | bytes 98312 | tf_op jit(solution)/shard_map/ppermute | solution.py:28
  178.3 6.1 %collective-permute-start.16 = (f32[8,1024]{1,0:T(8,128)S(1)}, f32[8,1024]{1,0:T(8,128)S(1)}, u32[]{:S(2)}, u32[]{:S(2)}) collective-permute-start(f32[8,1024]{1,0:T(8,128)S(1)} %collective-permute-done.15), channel_id=1, source_target_pairs={{0,1},{1,2},{2,3},{3,0},{4,5},{5,6},{6,7},{7,4},{8,9},{9,10},{10,1... | collective-permute-start | bytes 98312 | tf_op jit(solution)/shard_map/ppermute | solution.py:28
  184.3 5.7 %collective-permute-start.17 = (f32[8,1024]{1,0:T(8,128)S(1)}, f32[8,1024]{1,0:T(8,128)S(1)}, u32[]{:S(2)}, u32[]{:S(2)}) collective-permute-start(f32[8,1024]{1,0:T(8,128)S(1)} %collective-permute-done.16), channel_id=1, source_target_pairs={{0,1},{1,2},{2,3},{3,0},{4,5},{5,6},{6,7},{7,4},{8,9},{9,10},{10,1... | collective-permute-start | bytes 98312 | tf_op jit(solution)/shard_map/ppermute | solution.py:28
  192.4 5.2 %collective-permute-start.20 = (f32[32,128]{1,0:T(8,128)S(1)}, f32[32,128]{1,0:T(8,128)S(1)}, u32[]{:S(2)}, u32[]{:S(2)}) collective-permute-start(f32[32,128]{1,0:T(8,128)S(1)} %fusion.63), channel_id=1, source_target_pairs={{0,4},{1,5},{2,6},{3,7},{4,0},{5,1},{6,2},{7,3},{8,12},{9,13},{10,... | collective-permute-start | bytes 49160 | tf_op jit(solution)/shard_map/ppermute | solution.py:40
  192.4 6.0 %collective-permute-start.21 = (f32[32,128]{1,0:T(8,128)S(1)}, f32[32,128]{1,0:T(8,128)S(1)}, u32[]{:S(2)}, u32[]{:S(2)}) collective-permute-start(f32[32,128]{1,0:T(8,128)S(1)} %fusion.59), channel_id=1, source_target_pairs={{0,8},{1,9},{2,10},{3,11},{4,12},{5,13},{6,14},{7,15},{8,0},{9,1},... | collective-permute-start | bytes 49160 | tf_op jit(solution)/shard_map/ppermute | solution.py:40
  252.6 6.4 %collective-permute-start.22 = (f32[32,128]{1,0:T(8,128)S(1)}, f32[32,128]{1,0:T(8,128)S(1)}, u32[]{:S(2)}, u32[]{:S(2)}) collective-permute-start(f32[32,128]{1,0:T(8,128)S(1)} %fusion.70), channel_id=1, source_target_pairs={{0,1},{1,0},{2,3},{3,2},{4,5},{5,4},{6,7},{7,6},{8,9},{9,8},{10,11... | collective-permute-start | bytes 49160 | tf_op jit(solution)/shard_map/ppermute | solution.py:40
  252.7 7.2 %collective-permute-start.23 = (f32[32,128]{1,0:T(8,128)S(1)}, f32[32,128]{1,0:T(8,128)S(1)}, u32[]{:S(2)}, u32[]{:S(2)}) collective-permute-start(f32[32,128]{1,0:T(8,128)S(1)} %fusion.66), channel_id=1, source_target_pairs={{0,2},{1,3},{2,0},{3,1},{4,6},{5,7},{6,4},{7,5},{8,10},{9,11},{10,... | collective-permute-start | bytes 49160 | tf_op jit(solution)/shard_map/ppermute | solution.py:40
  254.8 5.9 %collective-permute-start.24 = (f32[32,128]{1,0:T(8,128)S(1)}, f32[32,128]{1,0:T(8,128)S(1)}, u32[]{:S(2)}, u32[]{:S(2)}) collective-permute-start(f32[32,128]{1,0:T(8,128)S(1)} %fusion.62), channel_id=1, source_target_pairs={{0,4},{1,5},{2,6},{3,7},{4,0},{5,1},{6,2},{7,3},{8,12},{9,13},{10,... | collective-permute-start | bytes 49160 | tf_op jit(solution)/shard_map/ppermute | solution.py:40
  254.8 6.7 %collective-permute-start.25 = (f32[32,128]{1,0:T(8,128)S(1)}, f32[32,128]{1,0:T(8,128)S(1)}, u32[]{:S(2)}, u32[]{:S(2)}) collective-permute-start(f32[32,128]{1,0:T(8,128)S(1)} %fusion.58), channel_id=1, source_target_pairs={{0,8},{1,9},{2,10},{3,11},{4,12},{5,13},{6,14},{7,15},{8,0},{9,1},... | collective-permute-start | bytes 49160 | tf_op jit(solution)/shard_map/ppermute | solution.py:40
  (34 other events, 772.1 us)
Sparse Core Ops, SparseCore 0:
  36.8 16.4 reduce-scatter.2
  150.3 19.8 reduce-scatter.4
